TPU v7x, 512 devices: a whole 4x4x16 slice. The times are simulated.
512 devices in a mesh: dom: 64 (over z_hi, x, y, core), lag: 8 (over z_lo).
Axes of the slice: x: 4, y: 4, z: 16 (z_hi: 2, z_lo: 8; z = z_hi * 8 + z_lo), core: 2. Of those that a mesh axis runs over, the one named last changes fastest.
Arguments:
- delayed_crowd_history: bfloat16 [8, 64, 2048, 128], P('lag', None, 'dom'), may hold values from -6 to 6
- predicted_crowd_array: bfloat16 [64, 2048, 128], P('lag', 'dom'), may hold values from -40 to 40
- probe_target_spot: int32 [1024, 256], P('dom'), may hold values from 0 to 255
- alive_probe_places: int32 [1024], P('dom'), may hold values from 64 to 256, as said below
- probed_heat_levels: float32 [1024, 256], P('dom'), may hold values from -6 to 6
- probe_reciprocal_spread: float32 [1024, 256], P('dom'), may hold values from 0.1 to 1.6
- decay_extent_squares: int32 [1024], P('dom'), may hold values from 16 to 32
Outputs:
- smoothed: bfloat16 [8, 64, 2048, 128], P('lag', None, 'dom')
Inputs may be any that keep to these rules, and one draw needn't show every extreme that they name: `alive_probe_places`: live observations of a patch occupy its first slots.
All inputs are finite; a program needn't handle non-finite values.
Results may differ from a plain program's by a relative error of at most 0.0062.
Values may be sent and summed in bfloat16 or wider, within the bound.
A program may use at most 64 MiB of HBM per device.

v0:
```python
import jax
import jax.numpy as jnp
from jax import lax
from jax.sharding import PartitionSpec as P

PATCH = 16
NS_STEPS = 4
REACH = 2


def padded_2(block, sides, width):
    for axis, dim in sides:
        count = lax.axis_size(axis)
        forward = [(i, i + 1) for i in range(count - 1)]
        backward = [(target, source) for source, target in forward]
        low = lax.ppermute(
            lax.slice_in_dim(block, block.shape[dim] - width, None, axis=dim), axis, forward
        )
        high = lax.ppermute(lax.slice_in_dim(block, 0, width, axis=dim), axis, backward)
        block = jnp.concatenate([low, block, high], axis=dim)
    return block


def inverse_root(gram_part, right_side):
    crowd_members_number = gram_part.shape[-1]
    identity = jnp.eye(crowd_members_number, dtype=jnp.float32)
    frobenius = jnp.sqrt(jnp.sum(gram_part * gram_part, axis=(1, 2)))
    bound_value = crowd_members_number - 1.0 + frobenius
    iterate = (gram_part + (crowd_members_number - 1.0) * identity) / bound_value[:, None, None]
    root_iter = jnp.broadcast_to(identity, gram_part.shape)
    for sweep_index in range(NS_STEPS):
        correction = 1.5 * identity - 0.5 * jnp.matmul(
            root_iter, iterate, precision=lax.Precision.HIGHEST
        )
        iterate = jnp.matmul(iterate, correction, precision=lax.Precision.HIGHEST)
        root_iter = jnp.matmul(correction, root_iter, precision=lax.Precision.HIGHEST)
    inner_prod = jnp.matmul(root_iter, right_side[:, :, None], precision=lax.Precision.HIGHEST)
    mean_weights = (
        jnp.matmul(root_iter, inner_prod, precision=lax.Precision.HIGHEST)[:, :, 0]
        / bound_value[:, None]
    )
    spread = jnp.sqrt(crowd_members_number - 1.0) / jnp.sqrt(bound_value)
    return (spread[:, None, None] * root_iter + mean_weights[:, :, None]).astype(jnp.bfloat16)


def local_gram(padded, radius, crowd_members_number, patch_rows, patch_cols):
    group_size = padded.shape[3]
    reach_width = 2 * REACH + 1
    col_base = jnp.repeat(
        (jnp.arange(reach_width, dtype=jnp.int32) - REACH) * PATCH, group_size
    ).astype(jnp.float32)
    gram_sum = jnp.zeros(
        (patch_rows, patch_cols, crowd_members_number, crowd_members_number), jnp.float32
    )
    right_side = jnp.zeros((patch_rows, patch_cols, crowd_members_number), jnp.float32)
    for shift_row in range(reach_width):
        pieces = [
            padded[:, shift_row : shift_row + patch_rows, shift_col : shift_col + patch_cols, :]
            for shift_col in range(reach_width)
        ]
        stacked = jnp.concatenate(pieces, axis=3)
        anomaly_near = stacked[:crowd_members_number]
        weight_near = stacked[crowd_members_number].astype(jnp.float32)
        innov_near = stacked[crowd_members_number + 1].astype(jnp.float32)
        row_offset = (
            (shift_row - REACH) * PATCH
            + stacked[crowd_members_number + 2].astype(jnp.float32)
            - 7.5
        )
        col_offset = col_base + stacked[crowd_members_number + 3].astype(jnp.float32) - 7.5
        taper_weight = jnp.square(
            jnp.maximum(
                0.0, 1.0 - (jnp.square(row_offset) + jnp.square(col_offset)) / jnp.square(radius)
            )
        )
        scaled = (taper_weight * weight_near * anomaly_near.astype(jnp.float32)).astype(
            jnp.bfloat16
        )
        weighted = (taper_weight * innov_near).astype(jnp.bfloat16)
        gram_sum = gram_sum + jnp.einsum(
            "mxyo,nxyo->xymn", scaled, anomaly_near, preferred_element_type=jnp.float32
        )
        right_side = right_side + jnp.einsum(
            "mxyo,xyo->xym", anomaly_near, weighted, preferred_element_type=jnp.float32
        )
    return (gram_sum, right_side)


def shards(
    delayed_crowd_history,
    predicted_crowd_array,
    probe_target_spot,
    alive_probe_places,
    probed_heat_levels,
    probe_reciprocal_spread,
    decay_extent_squares,
):
    lag_total = lax.axis_size("lag")
    lag_rank = lax.axis_index("lag")
    crowd_share_part, tile_vertical_extent, tile_lateral_extent = predicted_crowd_array.shape
    patch_rows = tile_vertical_extent // PATCH
    patch_cols = tile_lateral_extent // PATCH
    patch_total = patch_rows * patch_cols
    slot_count = probe_target_spot.shape[1]
    group_size = slot_count // lag_total
    index_patch = jnp.arange(patch_total, dtype=jnp.int32)
    lattice_node_place = (
        ((index_patch // patch_cols)[:, None] * PATCH + probe_target_spot // PATCH)
        * tile_lateral_extent
        + (index_patch % patch_cols)[:, None] * PATCH
        + probe_target_spot % PATCH
    )
    probed_markers = jnp.take(
        predicted_crowd_array.reshape(crowd_share_part, tile_vertical_extent * tile_lateral_extent),
        lattice_node_place.reshape(-1),
        axis=1,
    )
    probed_markers = probed_markers.reshape(crowd_share_part, patch_rows, patch_cols, slot_count)
    received = lax.all_to_all(probed_markers, "lag", split_axis=3, concat_axis=0, tiled=True)
    crowd_members_number = received.shape[0]
    average_reading = jnp.sum(received, axis=0, dtype=jnp.float32) / crowd_members_number
    obs_anomaly = (received.astype(jnp.float32) - average_reading).astype(jnp.bfloat16)
    slot_start = lag_rank * group_size

    def gather_fraction(table):
        piece = lax.dynamic_slice_in_dim(table, slot_start, group_size, 1)
        return piece.reshape(patch_rows, patch_cols, group_size)

    slot_index = slot_start + jnp.arange(group_size, dtype=jnp.int32)
    usable_entry = (slot_index[None, :] < alive_probe_places[:, None]).reshape(
        patch_rows, patch_cols, group_size
    )
    precision_share = gather_fraction(probe_reciprocal_spread)
    reading_fraction = gather_fraction(probed_heat_levels)
    cell_share = gather_fraction(probe_target_spot)
    obs_weight = jnp.where(usable_entry, precision_share, 0.0).astype(jnp.bfloat16)
    departure_vector = jnp.where(
        usable_entry, precision_share * (reading_fraction - average_reading), 0.0
    ).astype(jnp.bfloat16)
    placed = jnp.stack(
        [
            obs_weight,
            departure_vector,
            (cell_share // PATCH).astype(jnp.bfloat16),
            (cell_share % PATCH).astype(jnp.bfloat16),
        ],
        0,
    )
    combined = jnp.concatenate([obs_anomaly, placed], 0)
    extended = padded_2(combined, (("dom", 1),), REACH)
    padded = jnp.pad(extended, ((0, 0), (0, 0), (REACH, REACH), (0, 0)))
    radius = decay_extent_squares.reshape(patch_rows, patch_cols, 1).astype(jnp.float32)
    gram_sum, right_side = local_gram(padded, radius, crowd_members_number, patch_rows, patch_cols)
    gram_flat = gram_sum.reshape(patch_total, crowd_members_number, crowd_members_number)
    rhs_flat = right_side.reshape(patch_total, crowd_members_number)
    gram_all, rhs_all = lax.psum((gram_flat, rhs_flat), "lag")
    transform = inverse_root(gram_all, rhs_all)
    lag_state = delayed_crowd_history[0]
    lag_mean = jnp.sum(lag_state, axis=0, dtype=jnp.float32) / crowd_members_number
    lag_anomaly = (lag_state.astype(jnp.float32) - lag_mean).astype(jnp.bfloat16)
    patch_grid = lag_anomaly.reshape(crowd_members_number, patch_rows, PATCH, patch_cols, PATCH)
    mixing = transform.reshape(patch_rows, patch_cols, crowd_members_number, crowd_members_number)
    updated = jnp.einsum(
        "maibj,abmn->naibj", patch_grid, mixing, preferred_element_type=jnp.float32
    )
    result = (
        updated.reshape(crowd_members_number, tile_vertical_extent, tile_lateral_extent) + lag_mean
    )
    return result.astype(jnp.bfloat16)[None]


def solution(mesh):
    in_specs = (
        P("lag", None, "dom", None),
        P("lag", "dom", None),
        P("dom", None),
        P("dom"),
        P("dom", None),
        P("dom", None),
        P("dom"),
    )
    out_specs = P("lag", None, "dom", None)
    return jax.shard_map(shards, mesh=mesh, in_specs=in_specs, out_specs=out_specs, check_vma=False)
```

profile of v0, /device:TPU:2, one launch (start us, length us, event | category | flops | bytes accessed | tf_op | source)
XLA Modules:
  0.0 256.4 jit_solution(7928711825052308144)
XLA Ops:
  8.2 1.3 copy.242
  9.5 12.1 %gather_fusion = bf16[4096,8]{1,0:T(8,128)(2,1)S(1)} fusion(bf16[8,4096]{0,1:T(8,128)(2,1)S(1)} %bitcast.330, s32[4096]{0:T(1024)S(1)} %broadcast_clamp_fusion), kind=kCustom, calls=%fused_computation | custom fusion | bytes 147456 | tf_op jit(solution)/shard_map/jit(_take)/gather | solution.py:113
  21.6 1.5 copy.243
  23.6 1.0 fusion.165
  24.7 1.7 reshape.455
  26.4 12.5 %all-to-all-start = ((bf16[8,2,2048]{2,1,0:T(2,128)(2,1)}), bf16[8,2,2048]{2,1,0:T(2,128)(2,1)S(1)}, u32[]{:S(2)}, u32[]{:S(2)}) async-start(bf16[8,2,2048]{2,1,0:T(2,128)(2,1)} %reshape.455), calls=%async_computation | async-start | bytes 131072 | tf_op jit(solution)/shard_map/all_to_all | solution.py:119
  42.3 7.5 %all-to-all-done = bf16[8,2,2048]{2,1,0:T(2,128)(2,1)S(1)} async-done(((bf16[8,2,2048]{2,1,0:T(2,128)(2,1)}), bf16[8,2,2048]{2,1,0:T(2,128)(2,1)S(1)}, u32[]{:S(2)}, u32[]{:S(2)}) %all-to-all-start) | async-done | bytes 65568 | tf_op jit(solution)/shard_map/all_to_all | solution.py:119
  49.8 1.2 reshape.456
  51.0 2.0 convert_reduce_fusion
  53.3 1.0 copy.283
  54.7 1.9 collective-permute-start
  56.6 5.9 %collective-permute-start.1 = (bf16[68,2,8,32]{3,2,1,0:T(8,128)(2,1)S(1)}, bf16[68,2,8,32]{3,2,1,0:T(8,128)(2,1)S(1)}, u32[]{:S(2)}, u32[]{:S(2)}) collective-permute-start(bf16[68,2,8,32]{3,2,1,0:T(8,128)(2,1)S(1)} %constant_dynamic-update-slice_fusion), channel_id=1, source_target_pairs={{8,0},{16,8},{24,16},{32,24},{40,32},{48,40},{56,48},{64,56},{72,6... | collective-permute-start | bytes 208904 | tf_op jit(solution)/shard_map/ppermute | solution.py:19
  62.6 2.1 collective-permute-done
  64.7 1.8 collective-permute-done.1
  67.2 2.7 %fusion.164 = (bf16[68,2,8,32]{3,2,1,0:T(8,128)(2,1)}, bf16[68,2,8,32]{3,2,1,0:T(8,128)(2,1)}, bf16[68,2,8,32]{3,2,1,0:T(8,128)(2,1)}, bf16[68,2,8,32]{3,2,1,0:T...) fusion(bf16[68,6,12,32]{3,2,1,0:T(8,128)(2,1)S(1)} %fusion.5), kind=kLoop, calls=%fused_computation.253 | loop fusion | bytes 2646016 | tf_op jit(solution)/shard_map/slice | solution.py:58
  72.5 1.6 concatenate.29
  75.6 1.6 concatenate.31
  78.0 1.5 concatenate.32
  80.4 1.7 concatenate.34
  82.9 2.4 concatenate.35
  85.4 1.1 slice.239
  86.5 1.6 fusion.157
  92.9 1.2 convolution_add_fusion
  94.2 1.3 fusion.23
  95.5 26.8 %psum.15 = f32[16,64]{1,0:T(8,128)S(1)} all-reduce(f32[16,64]{1,0:T(8,128)S(1)} %add_bitcast_fusion), channel_id=1, replica_groups=mesh['dom'=64,'lag'=8] {'lag'}, use_global_device_ids=true, to_apply=%region_4.5 | all-reduce | flops 1024 | bytes 8192 | tf_op jit(solution)/shard_map/psum | solution.py:156
  122.3 111.9 %all-reduce.3.cloned.1.call-done = f32[16,64,64]{2,1,0:T(8,128)} async-done(((f32[16,64,64]{2,1,0:T(8,128)}), f32[16,64,64]{2,1,0:T(8,128)}) %all-reduce.3.cloned.1.call-update) | async-done | bytes 262160 | tf_op jit(solution)/shard_map/psum | solution.py:156
  234.2 1.3 multiply_reduce_fusion
  235.5 1.7 fusion.9
  243.8 0.9 convolution_bitcast_fusion.1
  244.7 0.9 fusion.171
  246.0 0.9 convolution_bitcast_fusion
  247.9 1.6 copy.266
  (106 shorter events, 25.8 us)
Async XLA Ops:
  23.1 15.8 %copy-start.15 = (s32[16]{0:T(128)S(1)}, s32[16]{0:T(128)}, u32[]{:S(2)}) copy-start(s32[16]{0:T(128)} %param.13) | copy-start | bytes 196
  23.1 15.8 %copy-start.7 = (bf16[1,64,32,128]{3,2,1,0:T(8,128)(2,1)S(1)}, bf16[1,64,32,128]{3,2,1,0:T(8,128)(2,1)}, u32[]{:S(2)}) copy-start(bf16[1,64,32,128]{3,2,1,0:T(8,128)(2,1)} %param.7) | copy-start | bytes 1572868
  24.6 15.4 %copy-start.16 = (s32[16]{0:T(128)S(1)}, s32[16]{0:T(128)}, u32[]{:S(2)}) copy-start(s32[16]{0:T(128)} %param.10) | copy-start | bytes 196
  26.4 23.4 %all-to-all-start = ((bf16[8,2,2048]{2,1,0:T(2,128)(2,1)}), bf16[8,2,2048]{2,1,0:T(2,128)(2,1)S(1)}, u32[]{:S(2)}, u32[]{:S(2)}) async-start(bf16[8,2,2048]{2,1,0:T(2,128)(2,1)} %reshape.455), calls=%async_computation | async-start | bytes 131072 | tf_op jit(solution)/shard_map/all_to_all | solution.py:119
  38.9 195.3 %all-reduce.3.cloned.1.call-start = ((), (), s32[]{:S(2)}) async-start(), calls=%async_computation.1 | async-start | bytes 1048576 | tf_op jit(solution)/shard_map/psum | solution.py:156
  51.0 3.3 %copy-start.11 = (f32[16,256]{1,0:T(8,128)S(1)}, f32[16,256]{1,0:T(8,128)}, u32[]{:S(2)}) copy-start(f32[16,256]{1,0:T(8,128)} %param.12) | copy-start | bytes 49156
  51.0 3.4 %copy-start.14 = (f32[16,256]{1,0:T(8,128)S(1)}, f32[16,256]{1,0:T(8,128)}, u32[]{:S(2)}) copy-start(f32[16,256]{1,0:T(8,128)} %param.11) | copy-start | bytes 49156
  51.0 3.5 %copy-start.9 = (s32[16,256]{1,0:T(8,128)S(1)}, s32[16,256]{1,0:T(8,128)}, u32[]{:S(2)}) copy-start(s32[16,256]{1,0:T(8,128)} %param.9) | copy-start | bytes 49156
  54.7 10.0 %collective-permute-start = (bf16[68,2,8,32]{3,2,1,0:T(8,128)(2,1)S(1)}, bf16[68,2,8,32]{3,2,1,0:T(8,128)(2,1)S(1)}, u32[]{:S(2)}, u32[]{:S(2)}) collective-permute-start(bf16[68,2,8,32]{3,2,1,0:T(8,128)(2,1)S(1)} %constant_dynamic-update-slice_fusion), channel_id=1, source_target_pairs={{0,8},{8,16},{16,24},{24,32},{32,40},{40,48},{48,56},{56,64},{64,7... | collective-permute-start | bytes 208904 | tf_op jit(solution)/shard_map/ppermute | solution.py:16
  56.6 9.8 %collective-permute-start.1 = (bf16[68,2,8,32]{3,2,1,0:T(8,128)(2,1)S(1)}, bf16[68,2,8,32]{3,2,1,0:T(8,128)(2,1)S(1)}, u32[]{:S(2)}, u32[]{:S(2)}) collective-permute-start(bf16[68,2,8,32]{3,2,1,0:T(8,128)(2,1)S(1)} %constant_dynamic-update-slice_fusion), channel_id=1, source_target_pairs={{8,0},{16,8},{24,16},{32,24},{40,32},{48,40},{56,48},{64,56},{72,6... | collective-permute-start | bytes 208904 | tf_op jit(solution)/shard_map/ppermute | solution.py:19
  66.4 8.3 %copy-start.1 = (bf16[68,2,8,32]{3,2,1,0:T(8,128)(2,1)}, bf16[68,2,8,32]{3,2,1,0:T(8,128)(2,1)S(1)}, u32[]{:S(2)}) copy-start(bf16[68,2,8,32]{3,2,1,0:T(8,128)(2,1)S(1)} %collective-permute-done.1) | copy-start | bytes 208900
  74.7 3.3 %copy-start.6 = (bf16[68,2,8,32]{3,2,1,0:T(8,128)(2,1)S(1)}, bf16[68,2,8,32]{3,2,1,0:T(8,128)(2,1)}, u32[]{:S(2)}) copy-start(bf16[68,2,8,32]{3,2,1,0:T(8,128)(2,1)} %get-tuple-element.15) | copy-start | bytes 208900
  85.4 4.5 %copy-start = (bf16[68,2,8,160]{3,2,1,0:T(8,128)(2,1)S(1)}, bf16[68,2,8,160]{3,2,1,0:T(8,128)(2,1)}, u32[]{:S(2)}) copy-start(bf16[68,2,8,160]{3,2,1,0:T(8,128)(2,1)} %concatenate.35) | copy-start | bytes 1044484
  86.5 6.4 %copy-start.4 = (bf16[64,2,8,160]{3,2,1,0:T(8,128)(2,1)}, bf16[64,2,8,160]{3,2,1,0:T(8,128)(2,1)S(1)}, u32[]{:S(2)}) copy-start(bf16[64,2,8,160]{3,2,1,0:T(8,128)(2,1)S(1)} %slice.239) | copy-start | bytes 983044
  88.1 2.0 copy-start.3
  90.1 1.0 copy-start.2
  90.8 1.1 copy-start.5
  92.5 1.7 copy-start.12
  92.9 2.6 copy-start.13
  92.9 142.6 %copy-start.10 = (f32[64,64]{1,0:T(8,128)S(1)}, f32[64,64]{1,0:T(8,128)}, u32[]{:S(2)}) copy-start(f32[64,64]{1,0:T(8,128)} %get-tuple-element.46) | copy-start | bytes 49156
  234.2 3.6 %copy-start.8 = (f32[16,64,64]{2,1,0:T(8,128)S(1)}, f32[16,64,64]{2,1,0:T(8,128)}, u32[]{:S(2)}) copy-start(f32[16,64,64]{2,1,0:T(8,128)} %all-reduce.3.cloned.1.call-done) | copy-start | bytes 786436
Sparse Core Ops, SparseCore 0:
  94.3 139.8 all-reduce.2
where the time goes:
time: 257 us; the launch traced here: 256 us
  waiting for transfers between devices  123 us (48%)
  local copies, waits for them, and re-layouts  41.4 us (16%)
  blocking collectives  26.8 us (10%)
  starting transfers between devices  20.4 us (8%)
  matrix products  16.5 us (6%)
  other arithmetic  14 us (5%)
  between operations  14 us (5%)
    psum x1, waiting for transfers between devices, shards(): gram_all, rhs_all = lax.psum((gram_flat, rhs_flat), 'lag')  112 us
    psum x1, blocking collectives, shards(): gram_all, rhs_all = lax.psum((gram_flat, rhs_flat), 'lag')  26.8 us
    gather x2, local copies, waits for them, and re-layouts, shards(): jnp.take(predicted_crowd_array.reshape(crowd_share_part, tile_vertical_ex...  13.6 us
    all_to_all x1, starting transfers between devices, shards(): lax.all_to_all(probed_markers, 'lag', split_axis=3, concat_axis=0, tiled=...  12.5 us
    concatenate x5, local copies, waits for them, and re-layouts, local_gram(): stacked = jnp.concatenate(pieces, axis=3)  8.81 us
    all_to_all x1, waiting for transfers between devices, shards(): lax.all_to_all(probed_markers, 'lag', split_axis=3, concat_axis=0, tiled=...  7.52 us
    ppermute x1, starting transfers between devices, padded_2(): lax.ppermute(lax.slice_in_dim(block, 0, width, axis=dim), axis, backward)  5.93 us
    unnamed x39, local copies, waits for them, and re-layouts  5.35 us
  transfers between devices with their start and end apart: 4, of which 4 were waited for; matrix products, arithmetic and copies ran while one was open for 2% of the time, Pallas kernels for 0%

commit v1 on v0

--- a/solution.py
+++ b/solution.py
@@ -116,7 +116,9 @@
         axis=1,
     )
     probed_markers = probed_markers.reshape(crowd_share_part, patch_rows, patch_cols, slot_count)
-    received = lax.all_to_all(probed_markers, "lag", split_axis=3, concat_axis=0, tiled=True)
+    parts = jnp.split(probed_markers, lax.axis_size("lag"), axis=3)
+    got = lax.all_to_all(jnp.stack(parts), "lag", 0, 0)
+    received = jnp.concatenate(got, axis=0)
     crowd_members_number = received.shape[0]
     average_reading = jnp.sum(received, axis=0, dtype=jnp.float32) / crowd_members_number
     obs_anomaly = (received.astype(jnp.float32) - average_reading).astype(jnp.bfloat16)

time: 257 us -> 249 us (0.969)
  other arithmetic: 14 us -> 9.9 us
  local copies, waits for them, and re-layouts: 41.4 us -> 37.7 us
    unnamed x39 -> x46, local copies, waits for them, and re-layouts: 5.35 us -> 4 us
where the time goes in v1:
time: 249 us
  waiting for transfers between devices  123 us (49%)
  local copies, waits for them, and re-layouts  37.7 us (15%)
  blocking collectives  26.8 us (11%)
  starting transfers between devices  20.4 us (8%)
  matrix products  16.5 us (7%)
  between operations  13.9 us (6%)
  other arithmetic  9.9 us (4%)
    psum x1, waiting for transfers between devices, shards(): gram_all, rhs_all = lax.psum((gram_flat, rhs_flat), 'lag')  112 us
    psum x1, blocking collectives, shards(): gram_all, rhs_all = lax.psum((gram_flat, rhs_flat), 'lag')  26.8 us
    all_to_all x1, starting transfers between devices, shards(): got = lax.all_to_all(jnp.stack(parts), 'lag', 0, 0)  12.7 us
    gather x2, local copies, waits for them, and re-layouts, shards(): jnp.take(predicted_crowd_array.reshape(crowd_share_part, tile_vertical_ex...  12.5 us
    concatenate x5, local copies, waits for them, and re-layouts, local_gram(): stacked = jnp.concatenate(pieces, axis=3)  8.8 us
    all_to_all x1, waiting for transfers between devices, shards(): got = lax.all_to_all(jnp.stack(parts), 'lag', 0, 0)  7.59 us
    ppermute x1, starting transfers between devices, padded_2(): lax.ppermute(lax.slice_in_dim(block, 0, width, axis=dim), axis, backward)  5.75 us
  transfers between devices with their start and end apart: 4, of which 4 were waited for; matrix products, arithmetic and copies ran while one was open for 2% of the time, Pallas kernels for 0%

profile of v1, /device:TPU:2, one launch (start us, length us, event | category | flops | bytes accessed | tf_op | source)
XLA Modules:
  0.0 248.7 jit_solution(9822094062889660259)
XLA Ops:
  6.5 0.9 compare_and_fusion
  7.5 1.3 copy.117
  8.8 12.1 %gather_fusion = bf16[4096,8]{1,0:T(8,128)(2,1)S(1)} fusion(bf16[8,4096]{0,1:T(8,128)(2,1)S(1)} %bitcast.352, s32[4096]{0:T(1024)S(1)} %broadcast_clamp_fusion), kind=kCustom, calls=%fused_computation | custom fusion | bytes 147456 | tf_op jit(solution)/shard_map/jit(_take)/gather | solution.py:113
  21.9 0.9 reshape.451
  22.8 12.7 %all-to-all-start = ((bf16[8,2,2048]{2,1,0:T(2,128)(2,1)}), bf16[8,2,2048]{2,1,0:T(2,128)(2,1)S(1)}, u32[]{:S(2)}, u32[]{:S(2)}) async-start(bf16[8,2,2048]{2,1,0:T(2,128)(2,1)} %reshape.451), calls=%async_computation | async-start | bytes 131072 | tf_op jit(solution)/shard_map/all_to_all | solution.py:120
  38.8 7.6 %all-to-all-done = bf16[8,2,2048]{2,1,0:T(2,128)(2,1)S(1)} async-done(((bf16[8,2,2048]{2,1,0:T(2,128)(2,1)}), bf16[8,2,2048]{2,1,0:T(2,128)(2,1)S(1)}, u32[]{:S(2)}, u32[]{:S(2)}) %all-to-all-start) | async-done | bytes 65568 | tf_op jit(solution)/shard_map/all_to_all | solution.py:120
  47.1 1.9 collective-permute-start
  49.0 5.8 %collective-permute-start.1 = (bf16[68,2,8,32]{3,2,1,0:T(8,128)(2,1)S(1)}, bf16[68,2,8,32]{3,2,1,0:T(8,128)(2,1)S(1)}, u32[]{:S(2)}, u32[]{:S(2)}) collective-permute-start(bf16[68,2,8,32]{3,2,1,0:T(8,128)(2,1)S(1)} %constant_dynamic-update-slice_fusion), channel_id=1, source_target_pairs={{8,0},{16,8},{24,16},{32,24},{40,32},{48,40},{56,48},{64,56},{72,6... | collective-permute-start | bytes 208904 | tf_op jit(solution)/shard_map/ppermute | solution.py:19
  54.8 2.3 collective-permute-done
  57.0 1.8 collective-permute-done.1
  59.6 2.8 %fusion.173 = (bf16[68,2,8,32]{3,2,1,0:T(8,128)(2,1)}, bf16[68,2,8,32]{3,2,1,0:T(8,128)(2,1)}, bf16[68,2,8,32]{3,2,1,0:T(8,128)(2,1)}, bf16[68,2,8,32]{3,2,1,0:T...) fusion(bf16[68,6,12,32]{3,2,1,0:T(8,128)(2,1)S(1)} %fusion.5), kind=kLoop, calls=%fused_computation.269 | loop fusion | bytes 2646016 | tf_op jit(solution)/shard_map/slice | solution.py:58
  64.9 1.6 concatenate.29
  67.2 0.9 pad_maximum_fusion
  68.0 1.6 concatenate.31
  69.7 0.8 slice.215
  70.5 1.5 concatenate.32
  72.9 1.7 concatenate.34
  75.4 2.4 concatenate.35
  77.8 1.1 slice.239
  78.9 1.6 fusion.165
  80.6 0.8 fusion.21
  81.4 0.9 fusion.146
  85.4 1.2 convolution_add_fusion
  86.6 1.3 fusion.23
  87.9 26.8 %psum.15 = f32[16,64]{1,0:T(8,128)S(1)} all-reduce(f32[16,64]{1,0:T(8,128)S(1)} %add_bitcast_fusion), channel_id=1, replica_groups=mesh['dom'=64,'lag'=8] {'lag'}, use_global_device_ids=true, to_apply=%region_3.4 | all-reduce | flops 1024 | bytes 8192 | tf_op jit(solution)/shard_map/psum | solution.py:158
  114.7 111.8 %all-reduce.3.cloned.1.call-done = f32[16,64,64]{2,1,0:T(8,128)} async-done(((f32[16,64,64]{2,1,0:T(8,128)}), f32[16,64,64]{2,1,0:T(8,128)}) %all-reduce.3.cloned.1.call-update) | async-done | bytes 262160 | tf_op jit(solution)/shard_map/psum | solution.py:158
  226.5 1.3 multiply_reduce_fusion
  227.8 1.7 fusion.9
  236.1 0.9 convolution_bitcast_fusion.1
  237.0 0.9 fusion.179
  238.3 0.9 convolution_bitcast_fusion
  240.2 1.6 copy.138
  (108 shorter events, 21.3 us)
Async XLA Ops:
  6.5 29.0 %copy-start.15 = (s32[16]{0:T(128)S(1)}, s32[16]{0:T(128)}, u32[]{:S(2)}) copy-start(s32[16]{0:T(128)} %param.13) | copy-start | bytes 196
  6.5 29.0 %copy-start.7 = (bf16[1,64,32,128]{3,2,1,0:T(8,128)(2,1)S(1)}, bf16[1,64,32,128]{3,2,1,0:T(8,128)(2,1)}, u32[]{:S(2)}) copy-start(bf16[1,64,32,128]{3,2,1,0:T(8,128)(2,1)} %param.7) | copy-start | bytes 1572868
  21.3 15.4 %copy-start.16 = (s32[16]{0:T(128)S(1)}, s32[16]{0:T(128)}, u32[]{:S(2)}) copy-start(s32[16]{0:T(128)} %param.10) | copy-start | bytes 196
  22.8 23.9 %copy-start.11 = (f32[16,256]{1,0:T(8,128)S(1)}, f32[16,256]{1,0:T(8,128)}, u32[]{:S(2)}) copy-start(f32[16,256]{1,0:T(8,128)} %param.12) | copy-start | bytes 49156
  22.8 24.0 %copy-start.14 = (f32[16,256]{1,0:T(8,128)S(1)}, f32[16,256]{1,0:T(8,128)}, u32[]{:S(2)}) copy-start(f32[16,256]{1,0:T(8,128)} %param.11) | copy-start | bytes 49156
  22.8 24.1 %copy-start.9 = (s32[16,256]{1,0:T(8,128)S(1)}, s32[16,256]{1,0:T(8,128)}, u32[]{:S(2)}) copy-start(s32[16,256]{1,0:T(8,128)} %param.9) | copy-start | bytes 49156
  22.8 23.6 %all-to-all-start = ((bf16[8,2,2048]{2,1,0:T(2,128)(2,1)}), bf16[8,2,2048]{2,1,0:T(2,128)(2,1)S(1)}, u32[]{:S(2)}, u32[]{:S(2)}) async-start(bf16[8,2,2048]{2,1,0:T(2,128)(2,1)} %reshape.451), calls=%async_computation | async-start | bytes 131072 | tf_op jit(solution)/shard_map/all_to_all | solution.py:120
  35.4 191.1 %all-reduce.3.cloned.1.call-start = ((), (), s32[]{:S(2)}) async-start(), calls=%async_computation.1 | async-start | bytes 1048576 | tf_op jit(solution)/shard_map/psum | solution.py:158
  47.1 10.0 %collective-permute-start = (bf16[68,2,8,32]{3,2,1,0:T(8,128)(2,1)S(1)}, bf16[68,2,8,32]{3,2,1,0:T(8,128)(2,1)S(1)}, u32[]{:S(2)}, u32[]{:S(2)}) collective-permute-start(bf16[68,2,8,32]{3,2,1,0:T(8,128)(2,1)S(1)} %constant_dynamic-update-slice_fusion), channel_id=1, source_target_pairs={{0,8},{8,16},{16,24},{24,32},{32,40},{40,48},{48,56},{56,64},{64,7... | collective-permute-start | bytes 208904 | tf_op jit(solution)/shard_map/ppermute | solution.py:16
  49.0 9.8 %collective-permute-start.1 = (bf16[68,2,8,32]{3,2,1,0:T(8,128)(2,1)S(1)}, bf16[68,2,8,32]{3,2,1,0:T(8,128)(2,1)S(1)}, u32[]{:S(2)}, u32[]{:S(2)}) collective-permute-start(bf16[68,2,8,32]{3,2,1,0:T(8,128)(2,1)S(1)} %constant_dynamic-update-slice_fusion), channel_id=1, source_target_pairs={{8,0},{16,8},{24,16},{32,24},{40,32},{48,40},{56,48},{64,56},{72,6... | collective-permute-start | bytes 208904 | tf_op jit(solution)/shard_map/ppermute | solution.py:19
  58.8 8.4 %copy-start.1 = (bf16[68,2,8,32]{3,2,1,0:T(8,128)(2,1)}, bf16[68,2,8,32]{3,2,1,0:T(8,128)(2,1)S(1)}, u32[]{:S(2)}) copy-start(bf16[68,2,8,32]{3,2,1,0:T(8,128)(2,1)S(1)} %collective-permute-done.1) | copy-start | bytes 208900
  67.2 3.3 %copy-start.6 = (bf16[68,2,8,32]{3,2,1,0:T(8,128)(2,1)S(1)}, bf16[68,2,8,32]{3,2,1,0:T(8,128)(2,1)}, u32[]{:S(2)}) copy-start(bf16[68,2,8,32]{3,2,1,0:T(8,128)(2,1)} %get-tuple-element.17) | copy-start | bytes 208900
  77.8 4.5 %copy-start = (bf16[68,2,8,160]{3,2,1,0:T(8,128)(2,1)S(1)}, bf16[68,2,8,160]{3,2,1,0:T(8,128)(2,1)}, u32[]{:S(2)}) copy-start(bf16[68,2,8,160]{3,2,1,0:T(8,128)(2,1)} %concatenate.35) | copy-start | bytes 1044484
  78.9 6.4 %copy-start.4 = (bf16[64,2,8,160]{3,2,1,0:T(8,128)(2,1)}, bf16[64,2,8,160]{3,2,1,0:T(8,128)(2,1)S(1)}, u32[]{:S(2)}) copy-start(bf16[64,2,8,160]{3,2,1,0:T(8,128)(2,1)S(1)} %slice.239) | copy-start | bytes 983044
  80.6 2.0 copy-start.3
  82.5 1.0 copy-start.2
  83.3 1.1 copy-start.5
  84.9 1.7 copy-start.12
  85.4 2.6 %copy-start.13 = (f32[2,8,1,64]{3,2,1,0:T(1,128)S(1)}, f32[2,8,1,64]{3,2,1,0:T(1,128)}, u32[]{:S(2)}) copy-start(f32[2,8,1,64]{3,2,1,0:T(1,128)} %fusion.21) | copy-start | bytes 12292
  85.4 142.5 %copy-start.10 = (f32[64,64]{1,0:T(8,128)S(1)}, f32[64,64]{1,0:T(8,128)}, u32[]{:S(2)}) copy-start(f32[64,64]{1,0:T(8,128)} %get-tuple-element.48) | copy-start | bytes 49156
  226.5 3.6 %copy-start.8 = (f32[16,64,64]{2,1,0:T(8,128)S(1)}, f32[16,64,64]{2,1,0:T(8,128)}, u32[]{:S(2)}) copy-start(f32[16,64,64]{2,1,0:T(8,128)} %all-reduce.3.cloned.1.call-done) | copy-start | bytes 786436
Sparse Core Ops, SparseCore 0:
  86.7 139.7 all-reduce.2
